TPU v7x, 512 devices: a whole 4x8x8 slice. The times are simulated.
512 devices in a mesh: ctx: 64 (over z, x, core), head: 8 (over y).
Axes of the slice: x: 4, y: 8, z: 8, core: 2. Of those that a mesh axis runs over, the one named last changes fastest.
Arguments:
- queries: bfloat16 [16384, 4096], P(('ctx', 'head')), may hold values from -6 to 6
- key_rows: bfloat16 [16384, 4096], P(('ctx', 'head')), may hold values from -6 to 6
- value_rows: bfloat16 [16384, 4096], P(('ctx', 'head')), may hold values from -6 to 6
- grad_out: bfloat16 [16384, 4096], P(('ctx', 'head')), may hold values from -6 to 6
Outputs:
- grad_query: bfloat16 [16384, 4096], P(('ctx', 'head'))
- grad_key: bfloat16 [16384, 4096], P(('ctx', 'head'))
- grad_value: bfloat16 [16384, 4096], P(('ctx', 'head'))
All inputs are finite; a program needn't handle non-finite values.
Results may differ from a plain program's by a relative error of at most 0.0021.
Values may be sent and summed in bfloat16 or wider, within the bound.
A program may use at most 128 MiB of HBM per device.

v0:
```python
import jax
import jax.numpy as jnp
from jax import lax
from jax.sharding import PartitionSpec as P

HEAD_DIM = 128
GROUP = 128


def exclusive_scans(forward_part, backward_part, axis):
    count = lax.axis_size(axis)
    fwd_total, fwd_excl = (forward_part, jnp.zeros_like(forward_part))
    bwd_total, bwd_excl = (backward_part, jnp.zeros_like(backward_part))
    shift = 1
    while shift < count:
        to_right = [(i, i + shift) for i in range(count - shift)]
        to_left = [(i + shift, i) for i in range(count - shift)]
        got_fwd = lax.ppermute(fwd_total, axis, to_right)
        got_bwd = lax.ppermute(bwd_total, axis, to_left)
        fwd_excl = fwd_excl + got_fwd
        bwd_excl = bwd_excl + got_bwd
        if shift * 2 < count:
            fwd_total = fwd_total + got_fwd
            bwd_total = bwd_total + got_bwd
        shift *= 2
    return (fwd_excl, bwd_excl)


def per_device(queries, key_rows, value_rows, grad_out):
    stacked = jnp.stack([queries, key_rows, value_rows, grad_out])
    q_all, k_all, v_all, d_all = lax.all_to_all(
        stacked, "head", split_axis=2, concat_axis=1, tiled=True
    )
    rows_here = q_all.shape[0]
    heads_here = q_all.shape[1] // HEAD_DIM
    scale = (HEAD_DIM * rows_here * lax.axis_size("ctx")) ** (-0.5)
    highest = lax.Precision.HIGHEST
    block = GROUP
    nblocks = rows_here // block
    shape_four = (nblocks, block, heads_here, HEAD_DIM)
    q_four = q_all.reshape(shape_four)
    k_four = k_all.reshape(shape_four)
    v_four = v_all.reshape(shape_four)
    d_four = d_all.reshape(shape_four)
    kv_blocks = jnp.einsum("ntha,nthb->nhab", v_four, k_four, preferred_element_type=jnp.float32)
    g_blocks = jnp.einsum("ntha,nthb->nhab", d_four, q_four, preferred_element_type=jnp.float32)
    kv_local = jnp.sum(kv_blocks, axis=0)
    g_local = jnp.sum(g_blocks, axis=0)
    kv_before, g_after = exclusive_scans(kv_local, g_local, "ctx")
    row_ids = lax.broadcasted_iota(jnp.int32, (nblocks, nblocks), 0)
    col_ids = lax.broadcasted_iota(jnp.int32, (nblocks, nblocks), 1)
    strict_lower = (col_ids < row_ids).astype(jnp.float32)
    strict_upper = (col_ids > row_ids).astype(jnp.float32)
    kv_in = kv_before[None] + jnp.einsum(
        "mn,nhab->mhab", strict_lower, kv_blocks, precision=highest
    )
    g_in = g_after[None] + jnp.einsum("mn,nhab->mhab", strict_upper, g_blocks, precision=highest)
    later = lax.broadcasted_iota(jnp.int32, (block, block), 0)
    earlier = lax.broadcasted_iota(jnp.int32, (block, block), 1)
    causal = (later >= earlier).astype(jnp.float32)
    scores = (
        jnp.einsum("nthd,nshd->nhts", q_four, k_four, preferred_element_type=jnp.float32)
        * (scale * causal)
    ).astype(jnp.bfloat16)
    dscores = (
        jnp.einsum("nthd,nshd->nhts", d_four, v_four, preferred_element_type=jnp.float32) * causal
    ).astype(jnp.bfloat16)
    k_float = k_four.astype(jnp.float32)
    v_float = v_four.astype(jnp.float32)
    d_float = d_four.astype(jnp.float32)
    grad_q = scale * (
        jnp.einsum("nhts,nshd->nthd", dscores, k_four, preferred_element_type=jnp.float32)
        + jnp.einsum("ntha,nhab->nthb", d_float, kv_in, precision=highest)
    )
    grad_k = scale * (
        jnp.einsum("nhts,nthd->nshd", dscores, q_four, preferred_element_type=jnp.float32)
        + jnp.einsum("ntha,nhab->nthb", v_float, g_in, precision=highest)
    )
    grad_v = jnp.einsum(
        "nhts,nthd->nshd", scores, d_four, preferred_element_type=jnp.float32
    ) + scale * jnp.einsum("nthb,nhab->ntha", k_float, g_in, precision=highest)
    flat_shape = (rows_here, heads_here * HEAD_DIM)
    grad_q = grad_q.reshape(flat_shape).astype(jnp.bfloat16)
    grad_k = grad_k.reshape(flat_shape).astype(jnp.bfloat16)
    grad_v = grad_v.reshape(flat_shape).astype(jnp.bfloat16)
    grads = jnp.stack([grad_q, grad_k, grad_v])
    result_q, result_k, result_v = lax.all_to_all(
        grads, "head", split_axis=1, concat_axis=2, tiled=True
    )
    return (result_q, result_k, result_v)


def solution(mesh):
    placed = (
        P(("ctx", "head"), None),
        P(("ctx", "head"), None),
        P(("ctx", "head"), None),
        P(("ctx", "head"), None),
    )
    return jax.shard_map(
        per_device,
        mesh=mesh,
        in_specs=placed,
        out_specs=(P(("ctx", "head"), None), P(("ctx", "head"), None), P(("ctx", "head"), None)),
        check_vma=False,
    )
```

profile of v0, /device:TPU:6, one launch (start us, length us, event | category | flops | bytes accessed | tf_op | source)
XLA Modules:
  0.0 192.5 jit_solution(13614894121044651994)
XLA Ops:
  2.0 4.7 %copy.93 = bf16[4,32,4096]{1,0,2:T(4,128)(2,1)} copy(bf16[4,32,4096]{2,1,0:T(8,128)(2,1)S(1)} %pad_maximum_fusion) | data formatting | bytes 2097152 | tf_op jit(solution)/shard_map/stack | solution.py:30
  6.6 7.0 %reshape.73 = bf16[8,2,32768]{2,1,0:T(2,128)(2,1)S(1)} reshape(bf16[4096,4,32]{2,1,0:T(4,128)(2,1)} %bitcast.57) | data formatting | bytes 2097152
  13.6 35.6 %all_to_all.30 = bf16[8,2,32768]{2,1,0:T(2,128)(2,1)S(1)} all-to-all(bf16[8,2,32768]{2,1,0:T(2,128)(2,1)S(1)} %reshape.73), channel_id=1, replica_groups=mesh['ctx'=64,'head'=8] {'head'}, dimensions={0} | all-to-all | bytes 2097152 | tf_op jit(solution)/shard_map/all_to_all | solution.py:31
  49.2 4.5 %reshape.74 = bf16[4096,4,32]{2,1,0:T(4,128)(2,1)} reshape(bf16[8,2,32768]{2,1,0:T(2,128)(2,1)S(1)} %all_to_all.30) | data formatting | bytes 2097152
  53.7 5.5 %copy.94 = bf16[4,32,8,512]{3,1,2,0:T(8,128)(2,1)S(1)} copy(bf16[4,32,8,512]{1,0,3,2:T(4,128)(2,1)} %bitcast.58) | data formatting | bytes 2097152 | tf_op jit(solution)/shard_map/all_to_all | solution.py:31
  59.8 1.9 collective-permute-start
  62.3 3.6 %collective-permute-start.6 = (f32[4,128,128]{2,1,0:T(8,128)S(1)}, f32[4,128,128]{2,1,0:T(8,128)S(1)}, u32[]{:S(2)}, u32[]{:S(2)}) collective-permute-start(f32[4,128,128]{2,1,0:T(8,128)S(1)} %get-tuple-element.10), channel_id=1, source_target_pairs={{8,0},{16,8},{24,16},{32,24},{40,32},{48,40},{56,48},{64,56},{72,6... | collective-permute-start | bytes 786440 | tf_op jit(solution)/shard_map/ppermute | solution.py:19
  65.9 1.5 collective-permute-done
  67.5 6.3 %collective-permute-start.1 = (f32[4,128,128]{2,1,0:T(8,128)S(1)}, f32[4,128,128]{2,1,0:T(8,128)S(1)}, u32[]{:S(2)}, u32[]{:S(2)}) collective-permute-start(f32[4,128,128]{2,1,0:T(8,128)S(1)} %add.88), channel_id=1, source_target_pairs={{0,16},{8,24},{16,32},{24,40},{32,48},{40,56},{48,64},{56,72},{64,... | collective-permute-start | bytes 786440 | tf_op jit(solution)/shard_map/ppermute | solution.py:18
  73.9 1.9 collective-permute-start.7
  75.8 1.9 collective-permute-done.1
  77.7 4.2 %collective-permute-start.2 = (f32[4,128,128]{2,1,0:T(8,128)S(1)}, f32[4,128,128]{2,1,0:T(8,128)S(1)}, u32[]{:S(2)}, u32[]{:S(2)}) collective-permute-start(f32[4,128,128]{2,1,0:T(8,128)S(1)} %add.90), channel_id=1, source_target_pairs={{0,32},{8,40},{16,48},{24,56},{32,64},{40,72},{48,80},{56,88},{64,... | collective-permute-start | bytes 786440 | tf_op jit(solution)/shard_map/ppermute | solution.py:18
  81.9 8.9 %collective-permute-done.7 = f32[4,128,128]{2,1,0:T(8,128)S(1)} collective-permute-done((f32[4,128,128]{2,1,0:T(8,128)S(1)}, f32[4,128,128]{2,1,0:T(8,128)S(1)}, u32[]{:S(2)}, u32[]{:S(2)}) %collective-permute-start.7) | collective-permute-done | bytes 262176 | tf_op jit(solution)/shard_map/ppermute | solution.py:19
  90.9 1.9 collective-permute-start.8
  92.8 4.3 %collective-permute-start.3 = (f32[4,128,128]{2,1,0:T(8,128)S(1)}, f32[4,128,128]{2,1,0:T(8,128)S(1)}, u32[]{:S(2)}, u32[]{:S(2)}) collective-permute-start(f32[4,128,128]{2,1,0:T(8,128)S(1)} %add.92), channel_id=1, source_target_pairs={{0,64},{8,72},{16,80},{24,88},{32,96},{40,104},{48,112},{56,120},{... | collective-permute-start | bytes 786440 | tf_op jit(solution)/shard_map/ppermute | solution.py:18
  97.2 5.4 %collective-permute-done.8 = f32[4,128,128]{2,1,0:T(8,128)S(1)} collective-permute-done((f32[4,128,128]{2,1,0:T(8,128)S(1)}, f32[4,128,128]{2,1,0:T(8,128)S(1)}, u32[]{:S(2)}, u32[]{:S(2)}) %collective-permute-start.8) | collective-permute-done | bytes 262176 | tf_op jit(solution)/shard_map/ppermute | solution.py:19
  103.9 7.7 %collective-permute-start.4 = (f32[4,128,128]{2,1,0:T(8,128)S(1)}, f32[4,128,128]{2,1,0:T(8,128)S(1)}, u32[]{:S(2)}, u32[]{:S(2)}) collective-permute-start(f32[4,128,128]{2,1,0:T(8,128)S(1)} %add.94), channel_id=1, source_target_pairs={{0,128},{8,136},{16,144},{24,152},{32,160},{40,168},{48,176},{56,1... | collective-permute-start | bytes 786440 | tf_op jit(solution)/shard_map/ppermute | solution.py:18
  113.3 2.3 %collective-permute-done.4 = f32[4,128,128]{2,1,0:T(8,128)S(1)} collective-permute-done((f32[4,128,128]{2,1,0:T(8,128)S(1)}, f32[4,128,128]{2,1,0:T(8,128)S(1)}, u32[]{:S(2)}, u32[]{:S(2)}) %collective-permute-start.4) | collective-permute-done | bytes 262176 | tf_op jit(solution)/shard_map/ppermute | solution.py:18
  115.7 19.5 %collective-permute-start.5 = (f32[4,128,128]{2,1,0:T(8,128)S(1)}, f32[4,128,128]{2,1,0:T(8,128)S(1)}, u32[]{:S(2)}, u32[]{:S(2)}) collective-permute-start(f32[4,128,128]{2,1,0:T(8,128)S(1)} %add.96), channel_id=1, source_target_pairs={{0,256},{8,264},{16,272},{24,280},{32,288},{40,296},{48,304},{56,3... | collective-permute-start | bytes 786440 | tf_op jit(solution)/shard_map/ppermute | solution.py:18
  138.6 2.4 %collective-permute-done.5 = f32[4,128,128]{2,1,0:T(8,128)S(1)} collective-permute-done((f32[4,128,128]{2,1,0:T(8,128)S(1)}, f32[4,128,128]{2,1,0:T(8,128)S(1)}, u32[]{:S(2)}, u32[]{:S(2)}) %collective-permute-start.5) | collective-permute-done | bytes 262176 | tf_op jit(solution)/shard_map/ppermute | solution.py:18
  141.1 1.4 broadcast_add_fusion.1
  144.1 9.8 %collective-permute-done.11 = f32[4,128,128]{2,1,0:T(8,128)} collective-permute-done((f32[4,128,128]{2,1,0:T(8,128)}, f32[4,128,128]{2,1,0:T(8,128)}, u32[]{:S(2)}, u32[]{:S(2)}) %collective-permute-start.11) | collective-permute-done | bytes 262176 | tf_op jit(solution)/shard_map/ppermute | solution.py:19
  155.2 1.4 broadcast_add_fusion
  159.8 30.3 %all_to_all.31 = bf16[3,256,512]{2,0,1:T(4,128)(2,1)S(1)} all-to-all(bf16[3,256,512]{2,0,1:T(4,128)(2,1)S(1)} %copy.117), channel_id=1, replica_groups=mesh['ctx'=64,'head'=8] {'head'}, dimensions={1} | all-to-all | bytes 1572864 | tf_op jit(solution)/shard_map/all_to_all | solution.py:87
  (59 shorter events, 17.5 us)
Async XLA Ops:
  59.8 7.7 %collective-permute-start = (f32[4,128,128]{2,1,0:T(8,128)S(1)}, f32[4,128,128]{2,1,0:T(8,128)S(1)}, u32[]{:S(2)}, u32[]{:S(2)}) collective-permute-start(f32[4,128,128]{2,1,0:T(8,128)S(1)} %get-tuple-element.12), channel_id=1, source_target_pairs={{0,8},{8,16},{16,24},{24,32},{32,40},{40,48},{48,56},{56,64},{64,7... | collective-permute-start | bytes 786440 | tf_op jit(solution)/shard_map/ppermute | solution.py:18
  62.3 11.5 %collective-permute-start.6 = (f32[4,128,128]{2,1,0:T(8,128)S(1)}, f32[4,128,128]{2,1,0:T(8,128)S(1)}, u32[]{:S(2)}, u32[]{:S(2)}) collective-permute-start(f32[4,128,128]{2,1,0:T(8,128)S(1)} %get-tuple-element.10), channel_id=1, source_target_pairs={{8,0},{16,8},{24,16},{32,24},{40,32},{48,40},{56,48},{64,56},{72,6... | collective-permute-start | bytes 786440 | tf_op jit(solution)/shard_map/ppermute | solution.py:19
  67.5 10.2 %collective-permute-start.1 = (f32[4,128,128]{2,1,0:T(8,128)S(1)}, f32[4,128,128]{2,1,0:T(8,128)S(1)}, u32[]{:S(2)}, u32[]{:S(2)}) collective-permute-start(f32[4,128,128]{2,1,0:T(8,128)S(1)} %add.88), channel_id=1, source_target_pairs={{0,16},{8,24},{16,32},{24,40},{32,48},{40,56},{48,64},{56,72},{64,... | collective-permute-start | bytes 786440 | tf_op jit(solution)/shard_map/ppermute | solution.py:18
  73.9 17.0 %collective-permute-start.7 = (f32[4,128,128]{2,1,0:T(8,128)S(1)}, f32[4,128,128]{2,1,0:T(8,128)S(1)}, u32[]{:S(2)}, u32[]{:S(2)}) collective-permute-start(f32[4,128,128]{2,1,0:T(8,128)S(1)} %add.101), channel_id=1, source_target_pairs={{16,0},{24,8},{32,16},{40,24},{48,32},{56,40},{64,48},{72,56},{80,... | collective-permute-start | bytes 786440 | tf_op jit(solution)/shard_map/ppermute | solution.py:19
  77.7 15.1 %collective-permute-start.2 = (f32[4,128,128]{2,1,0:T(8,128)S(1)}, f32[4,128,128]{2,1,0:T(8,128)S(1)}, u32[]{:S(2)}, u32[]{:S(2)}) collective-permute-start(f32[4,128,128]{2,1,0:T(8,128)S(1)} %add.90), channel_id=1, source_target_pairs={{0,32},{8,40},{16,48},{24,56},{32,64},{40,72},{48,80},{56,88},{64,... | collective-permute-start | bytes 786440 | tf_op jit(solution)/shard_map/ppermute | solution.py:18
  90.9 11.7 %collective-permute-start.8 = (f32[4,128,128]{2,1,0:T(8,128)S(1)}, f32[4,128,128]{2,1,0:T(8,128)S(1)}, u32[]{:S(2)}, u32[]{:S(2)}) collective-permute-start(f32[4,128,128]{2,1,0:T(8,128)S(1)} %add.103), channel_id=1, source_target_pairs={{32,0},{40,8},{48,16},{56,24},{64,32},{72,40},{80,48},{88,56},{96,... | collective-permute-start | bytes 786440 | tf_op jit(solution)/shard_map/ppermute | solution.py:19
  92.8 11.0 %collective-permute-start.3 = (f32[4,128,128]{2,1,0:T(8,128)S(1)}, f32[4,128,128]{2,1,0:T(8,128)S(1)}, u32[]{:S(2)}, u32[]{:S(2)}) collective-permute-start(f32[4,128,128]{2,1,0:T(8,128)S(1)} %add.92), channel_id=1, source_target_pairs={{0,64},{8,72},{16,80},{24,88},{32,96},{40,104},{48,112},{56,120},{... | collective-permute-start | bytes 786440 | tf_op jit(solution)/shard_map/ppermute | solution.py:18
  102.5 9.1 %copy-start = (f32[4,128,128]{2,1,0:T(8,128)}, f32[4,128,128]{2,1,0:T(8,128)S(1)}, u32[]{:S(2)}) copy-start(f32[4,128,128]{2,1,0:T(8,128)S(1)} %collective-permute-done.8) | copy-start | bytes 786436
  102.6 9.4 %collective-permute-start.9 = (f32[4,128,128]{2,1,0:T(8,128)S(1)}, f32[4,128,128]{2,1,0:T(8,128)S(1)}, u32[]{:S(2)}, u32[]{:S(2)}) collective-permute-start(f32[4,128,128]{2,1,0:T(8,128)S(1)} %add.105), channel_id=1, source_target_pairs={{64,0},{72,8},{80,16},{88,24},{96,32},{104,40},{112,48},{120,56},{... | collective-permute-start | bytes 786440 | tf_op jit(solution)/shard_map/ppermute | solution.py:19
  103.9 11.8 %collective-permute-start.4 = (f32[4,128,128]{2,1,0:T(8,128)S(1)}, f32[4,128,128]{2,1,0:T(8,128)S(1)}, u32[]{:S(2)}, u32[]{:S(2)}) collective-permute-start(f32[4,128,128]{2,1,0:T(8,128)S(1)} %add.94), channel_id=1, source_target_pairs={{0,128},{8,136},{16,144},{24,152},{32,160},{40,168},{48,176},{56,1... | collective-permute-start | bytes 786440 | tf_op jit(solution)/shard_map/ppermute | solution.py:18
  112.0 23.9 %copy-start.1 = (f32[4,128,128]{2,1,0:T(8,128)}, f32[4,128,128]{2,1,0:T(8,128)S(1)}, u32[]{:S(2)}) copy-start(f32[4,128,128]{2,1,0:T(8,128)S(1)} %collective-permute-done.9) | copy-start | bytes 786436
  112.0 23.8 %collective-permute-start.10 = (f32[4,128,128]{2,1,0:T(8,128)S(1)}, f32[4,128,128]{2,1,0:T(8,128)S(1)}, u32[]{:S(2)}, u32[]{:S(2)}) collective-permute-start(f32[4,128,128]{2,1,0:T(8,128)S(1)} %add.107), channel_id=1, source_target_pairs={{128,0},{136,8},{144,16},{152,24},{160,32},{168,40},{176,48},{184,... | collective-permute-start | bytes 786440 | tf_op jit(solution)/shard_map/ppermute | solution.py:19
  115.7 25.3 %collective-permute-start.5 = (f32[4,128,128]{2,1,0:T(8,128)S(1)}, f32[4,128,128]{2,1,0:T(8,128)S(1)}, u32[]{:S(2)}, u32[]{:S(2)}) collective-permute-start(f32[4,128,128]{2,1,0:T(8,128)S(1)} %add.96), channel_id=1, source_target_pairs={{0,256},{8,264},{16,272},{24,280},{32,288},{40,296},{48,304},{56,3... | collective-permute-start | bytes 786440 | tf_op jit(solution)/shard_map/ppermute | solution.py:18
  135.9 0.7 copy-start.2
  137.3 16.6 %collective-permute-start.11 = (f32[4,128,128]{2,1,0:T(8,128)}, f32[4,128,128]{2,1,0:T(8,128)}, u32[]{:S(2)}, u32[]{:S(2)}) collective-permute-start(f32[4,128,128]{2,1,0:T(8,128)} %add.109), channel_id=1, source_target_pairs={{256,0},{264,8},{272,16},{280,24},{288,32},{296,40},{304,48},{312,... | collective-permute-start | bytes 786440 | tf_op jit(solution)/shard_map/ppermute | solution.py:19
  155.2 3.8 %copy-start.3 = (bf16[1,256,512]{2,1,0:T(8,128)(2,1)S(1)}, bf16[1,256,512]{2,1,0:T(8,128)(2,1)}, u32[]{:S(2)}) copy-start(bf16[1,256,512]{2,1,0:T(8,128)(2,1)} %convert_element_type.70) | copy-start | bytes 786436
where the time goes:
time: 193 us
  blocking collectives  66 us (34%)
  starting transfers between devices  55.3 us (29%)
  waiting for transfers between devices  32.2 us (17%)
  local copies, waits for them, and re-layouts  27.6 us (14%)
  matrix products  6.56 us (3%)
  other arithmetic  3.85 us (2%)
    ppermute x6, starting transfers between devices, exclusive_scans(): got_fwd = lax.ppermute(fwd_total, axis, to_right)  43.9 us
    all_to_all x1, blocking collectives, per_device(): lax.all_to_all(stacked, 'head', split_axis=2, concat_axis=1, tiled=True)  35.6 us
    all_to_all x1, blocking collectives, per_device(): lax.all_to_all(grads, 'head', split_axis=1, concat_axis=2, tiled=True)  30.3 us
    ppermute x6, waiting for transfers between devices, exclusive_scans(): got_bwd = lax.ppermute(bwd_total, axis, to_left)  24.1 us
    unnamed x13, local copies, waits for them, and re-layouts  14.3 us
    ppermute x6, starting transfers between devices, exclusive_scans(): got_bwd = lax.ppermute(bwd_total, axis, to_left)  11.3 us
    ppermute x6, waiting for transfers between devices, exclusive_scans(): got_fwd = lax.ppermute(fwd_total, axis, to_right)  8.12 us
    all_to_all x1, local copies, waits for them, and re-layouts, per_device(): lax.all_to_all(stacked, 'head', split_axis=2, concat_axis=1, tiled=True)  5.51 us
  transfers between devices with their start and end apart: 12, of which 7 were waited for; matrix products, arithmetic and copies ran while one was open for 3% of the time, Pallas kernels for 0%

commit v1 on v0

--- a/solution.py
+++ b/solution.py
@@ -84,8 +84,9 @@
     grad_k = grad_k.reshape(flat_shape).astype(jnp.bfloat16)
     grad_v = grad_v.reshape(flat_shape).astype(jnp.bfloat16)
     grads = jnp.stack([grad_q, grad_k, grad_v])
-    result_q, result_k, result_v = lax.all_to_all(
-        grads, "head", split_axis=1, concat_axis=2, tiled=True
+    result_q, result_k, result_v = jnp.concatenate(
+        lax.all_to_all(jnp.stack(jnp.split(grads, lax.axis_size("head"), axis=1)), "head", 0, 0),
+        axis=2,
     )
     return (result_q, result_k, result_v)
 

time: 193 us -> 181 us (0.938)
  the two profiles are of different devices: /device:TPU:6 before, /device:TPU:64 now
where the time goes in v1:
time: 181 us; the launch traced here: 180 us
  blocking collectives  59.4 us (33%)
  starting transfers between devices  45.3 us (25%)
  waiting for transfers between devices  33.4 us (18%)
  local copies, waits for them, and re-layouts  28.1 us (16%)
  matrix products  8.75 us (5%)
  other arithmetic  3.79 us (2%)
    all_to_all x1, blocking collectives, per_device(): lax.all_to_all(stacked, 'head', split_axis=2, concat_axis=1, tiled=True)  35.6 us
    ppermute x6, starting transfers between devices, exclusive_scans(): got_fwd = lax.ppermute(fwd_total, axis, to_right)  31.4 us
    all_to_all x1, blocking collectives, per_device(): lax.all_to_all(jnp.stack(jnp.split(grads, lax.axis_size('head'), axis=1))...  23.7 us
    ppermute x6, waiting for transfers between devices, exclusive_scans(): got_bwd = lax.ppermute(bwd_total, axis, to_left)  23.3 us
    unnamed x24, local copies, waits for them, and re-layouts  14.5 us
    ppermute x6, starting transfers between devices, exclusive_scans(): got_bwd = lax.ppermute(bwd_total, axis, to_left)  13.9 us
    ppermute x6, waiting for transfers between devices, exclusive_scans(): got_fwd = lax.ppermute(fwd_total, axis, to_right)  10.1 us
    all_to_all x1, local copies, waits for them, and re-layouts, per_device(): lax.all_to_all(stacked, 'head', split_axis=2, concat_axis=1, tiled=True)  5.51 us
  transfers between devices with their start and end apart: 12, of which 9 were waited for; matrix products, arithmetic and copies ran while one was open for 6% of the time, Pallas kernels for 0%

profile of v1, /device:TPU:64, one launch (start us, length us, event | category | flops | bytes accessed | tf_op | source)
XLA Modules:
  0.0 179.8 jit_solution(17878139612484017616)
XLA Ops:
  2.0 4.7 %copy.98 = bf16[4,32,4096]{1,0,2:T(4,128)(2,1)} copy(bf16[4,32,4096]{2,1,0:T(8,128)(2,1)S(1)} %pad_maximum_fusion) | data formatting | bytes 2097152 | tf_op jit(solution)/shard_map/stack | solution.py:30
  6.6 7.0 %reshape.78 = bf16[8,2,32768]{2,1,0:T(2,128)(2,1)S(1)} reshape(bf16[4096,4,32]{2,1,0:T(4,128)(2,1)} %bitcast.87) | data formatting | bytes 2097152
  13.6 35.6 %all_to_all.20 = bf16[8,2,32768]{2,1,0:T(2,128)(2,1)S(1)} all-to-all(bf16[8,2,32768]{2,1,0:T(2,128)(2,1)S(1)} %reshape.78), channel_id=1, replica_groups=mesh['ctx'=64,'head'=8] {'head'}, dimensions={0} | all-to-all | bytes 2097152 | tf_op jit(solution)/shard_map/all_to_all | solution.py:31
  49.2 4.5 %reshape.79 = bf16[4096,4,32]{2,1,0:T(4,128)(2,1)} reshape(bf16[8,2,32768]{2,1,0:T(2,128)(2,1)S(1)} %all_to_all.20) | data formatting | bytes 2097152
  53.7 5.5 %copy.99 = bf16[4,32,8,512]{3,1,2,0:T(8,128)(2,1)S(1)} copy(bf16[4,32,8,512]{1,0,3,2:T(4,128)(2,1)} %bitcast.88) | data formatting | bytes 2097152 | tf_op jit(solution)/shard_map/all_to_all | solution.py:31
  59.9 1.9 %collective-permute-start.6 = (f32[4,128,128]{2,1,0:T(8,128)S(1)}, f32[4,128,128]{2,1,0:T(8,128)S(1)}, u32[]{:S(2)}, u32[]{:S(2)}) collective-permute-start(f32[4,128,128]{2,1,0:T(8,128)S(1)} %get-tuple-element.12), channel_id=1, source_target_pairs={{8,0},{16,8},{24,16},{32,24},{40,32},{48,40},{56,48},{64,56},{72,6... | collective-permute-start | bytes 786440 | tf_op jit(solution)/shard_map/ppermute | solution.py:19
  63.1 2.4 %collective-permute-start = (f32[4,128,128]{2,1,0:T(8,128)S(1)}, f32[4,128,128]{2,1,0:T(8,128)S(1)}, u32[]{:S(2)}, u32[]{:S(2)}) collective-permute-start(f32[4,128,128]{2,1,0:T(8,128)S(1)} %get-tuple-element.10), channel_id=1, source_target_pairs={{0,8},{8,16},{16,24},{24,32},{32,40},{40,48},{48,56},{56,64},{64,7... | collective-permute-start | bytes 786440 | tf_op jit(solution)/shard_map/ppermute | solution.py:18
  65.7 3.8 %collective-permute-start.7 = (f32[4,128,128]{2,1,0:T(8,128)S(1)}, f32[4,128,128]{2,1,0:T(8,128)S(1)}, u32[]{:S(2)}, u32[]{:S(2)}) collective-permute-start(f32[4,128,128]{2,1,0:T(8,128)S(1)} %add.101), channel_id=1, source_target_pairs={{16,0},{24,8},{32,16},{40,24},{48,32},{56,40},{64,48},{72,56},{80,... | collective-permute-start | bytes 786440 | tf_op jit(solution)/shard_map/ppermute | solution.py:19
  69.5 3.4 %collective-permute-done = f32[4,128,128]{2,1,0:T(8,128)S(1)} collective-permute-done((f32[4,128,128]{2,1,0:T(8,128)S(1)}, f32[4,128,128]{2,1,0:T(8,128)S(1)}, u32[]{:S(2)}, u32[]{:S(2)}) %collective-permute-start) | collective-permute-done | bytes 262176 | tf_op jit(solution)/shard_map/ppermute | solution.py:18
  72.9 1.9 %collective-permute-start.1 = (f32[4,128,128]{2,1,0:T(8,128)S(1)}, f32[4,128,128]{2,1,0:T(8,128)S(1)}, u32[]{:S(2)}, u32[]{:S(2)}) collective-permute-start(f32[4,128,128]{2,1,0:T(8,128)S(1)} %add.88), channel_id=1, source_target_pairs={{0,16},{8,24},{16,32},{24,40},{32,48},{40,56},{48,64},{56,72},{64,... | collective-permute-start | bytes 786440 | tf_op jit(solution)/shard_map/ppermute | solution.py:18
  76.1 3.7 %collective-permute-start.8 = (f32[4,128,128]{2,1,0:T(8,128)S(1)}, f32[4,128,128]{2,1,0:T(8,128)S(1)}, u32[]{:S(2)}, u32[]{:S(2)}) collective-permute-start(f32[4,128,128]{2,1,0:T(8,128)S(1)} %add.103), channel_id=1, source_target_pairs={{32,0},{40,8},{48,16},{56,24},{64,32},{72,40},{80,48},{88,56},{96,... | collective-permute-start | bytes 786440 | tf_op jit(solution)/shard_map/ppermute | solution.py:19
  79.8 5.3 %collective-permute-done.1 = f32[4,128,128]{2,1,0:T(8,128)S(1)} collective-permute-done((f32[4,128,128]{2,1,0:T(8,128)S(1)}, f32[4,128,128]{2,1,0:T(8,128)S(1)}, u32[]{:S(2)}, u32[]{:S(2)}) %collective-permute-start.1) | collective-permute-done | bytes 262176 | tf_op jit(solution)/shard_map/ppermute | solution.py:18
  85.2 1.9 %collective-permute-start.2 = (f32[4,128,128]{2,1,0:T(8,128)S(1)}, f32[4,128,128]{2,1,0:T(8,128)S(1)}, u32[]{:S(2)}, u32[]{:S(2)}) collective-permute-start(f32[4,128,128]{2,1,0:T(8,128)S(1)} %add.90), channel_id=1, source_target_pairs={{0,32},{8,40},{16,48},{24,56},{32,64},{40,72},{48,80},{56,88},{64,... | collective-permute-start | bytes 786440 | tf_op jit(solution)/shard_map/ppermute | solution.py:18
  87.1 5.4 %collective-permute-done.8 = f32[4,128,128]{2,1,0:T(8,128)S(1)} collective-permute-done((f32[4,128,128]{2,1,0:T(8,128)S(1)}, f32[4,128,128]{2,1,0:T(8,128)S(1)}, u32[]{:S(2)}, u32[]{:S(2)}) %collective-permute-start.8) | collective-permute-done | bytes 262176 | tf_op jit(solution)/shard_map/ppermute | solution.py:19
  92.5 1.9 %collective-permute-start.9 = (f32[4,128,128]{2,1,0:T(8,128)S(1)}, f32[4,128,128]{2,1,0:T(8,128)S(1)}, u32[]{:S(2)}, u32[]{:S(2)}) collective-permute-start(f32[4,128,128]{2,1,0:T(8,128)S(1)} %add.105), channel_id=1, source_target_pairs={{64,0},{72,8},{80,16},{88,24},{96,32},{104,40},{112,48},{120,56},{... | collective-permute-start | bytes 786440 | tf_op jit(solution)/shard_map/ppermute | solution.py:19
  94.5 1.4 collective-permute-done.2
  95.9 4.3 %collective-permute-start.3 = (f32[4,128,128]{2,1,0:T(8,128)S(1)}, f32[4,128,128]{2,1,0:T(8,128)S(1)}, u32[]{:S(2)}, u32[]{:S(2)}) collective-permute-start(f32[4,128,128]{2,1,0:T(8,128)S(1)} %add.92), channel_id=1, source_target_pairs={{0,64},{8,72},{16,80},{24,88},{32,96},{40,104},{48,112},{56,120},{... | collective-permute-start | bytes 786440 | tf_op jit(solution)/shard_map/ppermute | solution.py:18
  100.2 2.9 %collective-permute-done.9 = f32[4,128,128]{2,1,0:T(8,128)S(1)} collective-permute-done((f32[4,128,128]{2,1,0:T(8,128)S(1)}, f32[4,128,128]{2,1,0:T(8,128)S(1)}, u32[]{:S(2)}, u32[]{:S(2)}) %collective-permute-start.9) | collective-permute-done | bytes 262176 | tf_op jit(solution)/shard_map/ppermute | solution.py:19
  104.9 11.8 %collective-permute-start.4 = (f32[4,128,128]{2,1,0:T(8,128)S(1)}, f32[4,128,128]{2,1,0:T(8,128)S(1)}, u32[]{:S(2)}, u32[]{:S(2)}) collective-permute-start(f32[4,128,128]{2,1,0:T(8,128)S(1)} %add.94), channel_id=1, source_target_pairs={{0,128},{8,136},{16,144},{24,152},{32,160},{40,168},{48,176},{56,1... | collective-permute-start | bytes 786440 | tf_op jit(solution)/shard_map/ppermute | solution.py:18
  116.6 7.5 %collective-permute-done.10 = f32[4,128,128]{2,1,0:T(8,128)S(1)} collective-permute-done((f32[4,128,128]{2,1,0:T(8,128)S(1)}, f32[4,128,128]{2,1,0:T(8,128)S(1)}, u32[]{:S(2)}, u32[]{:S(2)}) %collective-permute-start.10) | collective-permute-done | bytes 262176 | tf_op jit(solution)/shard_map/ppermute | solution.py:19
  127.6 9.2 %collective-permute-start.5 = (f32[4,128,128]{2,1,0:T(8,128)}, f32[4,128,128]{2,1,0:T(8,128)}, u32[]{:S(2)}, u32[]{:S(2)}) collective-permute-start(f32[4,128,128]{2,1,0:T(8,128)} %add.96), channel_id=1, source_target_pairs={{0,256},{8,264},{16,272},{24,280},{32,288},{40,296},{48,304},{56,3... | collective-permute-start | bytes 786440 | tf_op jit(solution)/shard_map/ppermute | solution.py:18
  136.7 6.0 %collective-permute-done.11 = f32[4,128,128]{2,1,0:T(8,128)S(1)} collective-permute-done((f32[4,128,128]{2,1,0:T(8,128)S(1)}, f32[4,128,128]{2,1,0:T(8,128)S(1)}, u32[]{:S(2)}, u32[]{:S(2)}) %collective-permute-start.11) | collective-permute-done | bytes 262176 | tf_op jit(solution)/shard_map/ppermute | solution.py:19
  142.8 1.4 broadcast_add_fusion
  153.8 23.7 %all_to_all.21 = bf16[8,3,32,512]{3,2,1,0:T(8,128)(2,1)S(1)} all-to-all(bf16[8,3,32,512]{3,2,1,0:T(8,128)(2,1)S(1)} %fusion.34), channel_id=1, replica_groups=mesh['ctx'=64,'head'=8] {'head'}, dimensions={0} | all-to-all | bytes 1572864 | tf_op jit(solution)/shard_map/all_to_all | solution.py:88
  (69 shorter events, 21.7 us)
Async XLA Ops:
  59.9 5.8 %collective-permute-start.6 = (f32[4,128,128]{2,1,0:T(8,128)S(1)}, f32[4,128,128]{2,1,0:T(8,128)S(1)}, u32[]{:S(2)}, u32[]{:S(2)}) collective-permute-start(f32[4,128,128]{2,1,0:T(8,128)S(1)} %get-tuple-element.12), channel_id=1, source_target_pairs={{8,0},{16,8},{24,16},{32,24},{40,32},{48,40},{56,48},{64,56},{72,6... | collective-permute-start | bytes 786440 | tf_op jit(solution)/shard_map/ppermute | solution.py:19
  63.1 9.8 %collective-permute-start = (f32[4,128,128]{2,1,0:T(8,128)S(1)}, f32[4,128,128]{2,1,0:T(8,128)S(1)}, u32[]{:S(2)}, u32[]{:S(2)}) collective-permute-start(f32[4,128,128]{2,1,0:T(8,128)S(1)} %get-tuple-element.10), channel_id=1, source_target_pairs={{0,8},{8,16},{16,24},{24,32},{32,40},{40,48},{48,56},{56,64},{64,7... | collective-permute-start | bytes 786440 | tf_op jit(solution)/shard_map/ppermute | solution.py:18
  65.7 10.3 %collective-permute-start.7 = (f32[4,128,128]{2,1,0:T(8,128)S(1)}, f32[4,128,128]{2,1,0:T(8,128)S(1)}, u32[]{:S(2)}, u32[]{:S(2)}) collective-permute-start(f32[4,128,128]{2,1,0:T(8,128)S(1)} %add.101), channel_id=1, source_target_pairs={{16,0},{24,8},{32,16},{40,24},{48,32},{56,40},{64,48},{72,56},{80,... | collective-permute-start | bytes 786440 | tf_op jit(solution)/shard_map/ppermute | solution.py:19
  72.9 12.3 %collective-permute-start.1 = (f32[4,128,128]{2,1,0:T(8,128)S(1)}, f32[4,128,128]{2,1,0:T(8,128)S(1)}, u32[]{:S(2)}, u32[]{:S(2)}) collective-permute-start(f32[4,128,128]{2,1,0:T(8,128)S(1)} %add.88), channel_id=1, source_target_pairs={{0,16},{8,24},{16,32},{24,40},{32,48},{40,56},{48,64},{56,72},{64,... | collective-permute-start | bytes 786440 | tf_op jit(solution)/shard_map/ppermute | solution.py:18
  76.1 16.4 %collective-permute-start.8 = (f32[4,128,128]{2,1,0:T(8,128)S(1)}, f32[4,128,128]{2,1,0:T(8,128)S(1)}, u32[]{:S(2)}, u32[]{:S(2)}) collective-permute-start(f32[4,128,128]{2,1,0:T(8,128)S(1)} %add.103), channel_id=1, source_target_pairs={{32,0},{40,8},{48,16},{56,24},{64,32},{72,40},{80,48},{88,56},{96,... | collective-permute-start | bytes 786440 | tf_op jit(solution)/shard_map/ppermute | solution.py:19
  85.2 19.3 %copy-start.1 = (f32[4,128,128]{2,1,0:T(8,128)}, f32[4,128,128]{2,1,0:T(8,128)S(1)}, u32[]{:S(2)}) copy-start(f32[4,128,128]{2,1,0:T(8,128)S(1)} %collective-permute-done.1) | copy-start | bytes 786436
  85.2 10.7 %collective-permute-start.2 = (f32[4,128,128]{2,1,0:T(8,128)S(1)}, f32[4,128,128]{2,1,0:T(8,128)S(1)}, u32[]{:S(2)}, u32[]{:S(2)}) collective-permute-start(f32[4,128,128]{2,1,0:T(8,128)S(1)} %add.90), channel_id=1, source_target_pairs={{0,32},{8,40},{16,48},{24,56},{32,64},{40,72},{48,80},{56,88},{64,... | collective-permute-start | bytes 786440 | tf_op jit(solution)/shard_map/ppermute | solution.py:18
  92.5 10.6 %collective-permute-start.9 = (f32[4,128,128]{2,1,0:T(8,128)S(1)}, f32[4,128,128]{2,1,0:T(8,128)S(1)}, u32[]{:S(2)}, u32[]{:S(2)}) collective-permute-start(f32[4,128,128]{2,1,0:T(8,128)S(1)} %add.105), channel_id=1, source_target_pairs={{64,0},{72,8},{80,16},{88,24},{96,32},{104,40},{112,48},{120,56},{... | collective-permute-start | bytes 786440 | tf_op jit(solution)/shard_map/ppermute | solution.py:19
  95.9 29.6 %copy-start.2 = (f32[4,128,128]{2,1,0:T(8,128)}, f32[4,128,128]{2,1,0:T(8,128)S(1)}, u32[]{:S(2)}) copy-start(f32[4,128,128]{2,1,0:T(8,128)S(1)} %collective-permute-done.2) | copy-start | bytes 786436
  95.9 8.9 %collective-permute-start.3 = (f32[4,128,128]{2,1,0:T(8,128)S(1)}, f32[4,128,128]{2,1,0:T(8,128)S(1)}, u32[]{:S(2)}, u32[]{:S(2)}) collective-permute-start(f32[4,128,128]{2,1,0:T(8,128)S(1)} %add.92), channel_id=1, source_target_pairs={{0,64},{8,72},{16,80},{24,88},{32,96},{40,104},{48,112},{56,120},{... | collective-permute-start | bytes 786440 | tf_op jit(solution)/shard_map/ppermute | solution.py:18
  103.2 21.0 %collective-permute-start.10 = (f32[4,128,128]{2,1,0:T(8,128)S(1)}, f32[4,128,128]{2,1,0:T(8,128)S(1)}, u32[]{:S(2)}, u32[]{:S(2)}) collective-permute-start(f32[4,128,128]{2,1,0:T(8,128)S(1)} %add.107), channel_id=1, source_target_pairs={{128,0},{136,8},{144,16},{152,24},{160,32},{168,40},{176,48},{184,... | collective-permute-start | bytes 786440 | tf_op jit(solution)/shard_map/ppermute | solution.py:19
  104.8 20.7 %copy-start.3 = (f32[4,128,128]{2,1,0:T(8,128)}, f32[4,128,128]{2,1,0:T(8,128)S(1)}, u32[]{:S(2)}) copy-start(f32[4,128,128]{2,1,0:T(8,128)S(1)} %collective-permute-done.3) | copy-start | bytes 786436
  104.9 21.2 %collective-permute-start.4 = (f32[4,128,128]{2,1,0:T(8,128)S(1)}, f32[4,128,128]{2,1,0:T(8,128)S(1)}, u32[]{:S(2)}, u32[]{:S(2)}) collective-permute-start(f32[4,128,128]{2,1,0:T(8,128)S(1)} %add.94), channel_id=1, source_target_pairs={{0,128},{8,136},{16,144},{24,152},{32,160},{40,168},{48,176},{56,1... | collective-permute-start | bytes 786440 | tf_op jit(solution)/shard_map/ppermute | solution.py:18
  124.2 18.6 %collective-permute-start.11 = (f32[4,128,128]{2,1,0:T(8,128)S(1)}, f32[4,128,128]{2,1,0:T(8,128)S(1)}, u32[]{:S(2)}, u32[]{:S(2)}) collective-permute-start(f32[4,128,128]{2,1,0:T(8,128)S(1)} %add.109), channel_id=1, source_target_pairs={{256,0},{264,8},{272,16},{280,24},{288,32},{296,40},{304,48},{312,... | collective-permute-start | bytes 786440 | tf_op jit(solution)/shard_map/ppermute | solution.py:19
  126.1 0.7 copy-start.4
  127.6 22.4 %collective-permute-start.5 = (f32[4,128,128]{2,1,0:T(8,128)}, f32[4,128,128]{2,1,0:T(8,128)}, u32[]{:S(2)}, u32[]{:S(2)}) collective-permute-start(f32[4,128,128]{2,1,0:T(8,128)} %add.96), channel_id=1, source_target_pairs={{0,256},{8,264},{16,272},{24,280},{32,288},{40,296},{48,304},{56,3... | collective-permute-start | bytes 786440 | tf_op jit(solution)/shard_map/ppermute | solution.py:18
  146.1 5.2 %copy-start = (f32[2,4,128,128]{3,2,1,0:T(8,128)S(1)}, f32[2,4,128,128]{3,2,1,0:T(8,128)}, u32[]{:S(2)}) copy-start(f32[2,4,128,128]{3,2,1,0:T(8,128)} %get-tuple-element.11) | copy-start | bytes 1572868
